TPU v7x, 256 devices: a whole 4x4x8 slice. The times are simulated.
256 devices in a mesh: tok: 64 (over z, x, core), head: 4 (over y).
Axes of the slice: x: 4, y: 4, z: 8, core: 2. Of those that a mesh axis runs over, the one named last changes fastest.
Arguments:
- single: bfloat16 [2048, 768], P('tok'), may hold values from -6 to 6
- pair: bfloat16 [2048, 2048, 128], P('tok', 'head'), may hold values from -161 to 161
- atoms: bfloat16 [49152, 128], P('tok'), may hold values from -60 to 60
- atom_counts: int32 [2048], P('tok'), may hold values from 4 to 24, as said below
- w_atom: bfloat16 [128, 3, 128], P(None, None, 'head'), may hold values from -0.5 to 0.5
- w_atom_token: bfloat16 [128, 768], P('head'), may hold values from -6 to 6
- ln_gain: bfloat16 [768], replicated, may hold values from 0.099609375 to 1.8984375
- w_proj: bfloat16 [768, 4, 768], P(None, None, 'head'), may hold values from -0.21875 to 0.21875
- w_pair_bias: bfloat16 [128, 16], replicated, may hold values from -3.5 to 3.5
- w_out: bfloat16 [768, 768], P('head'), may hold values from -0.21875 to 0.21875
- ln_gain2: bfloat16 [768], replicated, may hold values from 0.099609375 to 1.8984375
- w_trans: bfloat16 [768, 2, 1536], P(None, None, 'head'), may hold values from -0.21875 to 0.21875
- w_trans_out: bfloat16 [1536, 768], P('head'), may hold values from -0.15625 to 0.15625
Outputs:
- refined: bfloat16 [2048, 768], P('tok', 'head')
- atom_mix: bfloat16 [128, 49152], P('head', 'tok')
Inputs may be any that keep to these rules, and one draw needn't show every extreme that they name: `atom_counts`: every token has 4 to 24 atoms; in every draw all tokens of some group of 32 have 24 atoms.
All inputs are finite; a program needn't handle non-finite values.
Results may differ from a plain program's by a relative error of at most 0.013.
Values may be sent and summed in bfloat16 or wider, within the bound.
No kernel may reach another device: no remote copies, remote signals or barrier semaphores. Data moves between devices by JAX's collectives and lax.ppermute only.
A program may use at most 64 MiB of HBM per device.

v0:
```python
import jax
import jax.numpy as jnp
from jax import lax
from jax.sharding import PartitionSpec as P

H = 16
AH = 4
QWIN = 32
KWIN = 128
norm_eps = 1e-05
masked_value = -1000000000.0


def from_behind(block, axis, distance):
    devices = range(lax.axis_size(axis))
    route = [(i - distance, i) for i in devices if i - distance in devices]
    return lax.ppermute(block, axis, route)


def sent_to_all(value, axis):
    copies = jnp.broadcast_to(value, (lax.axis_size(axis), *value.shape))
    return lax.all_to_all(copies, axis, split_axis=0, concat_axis=0, tiled=True)


def of_everyone(value, axis):
    return sent_to_all(value, axis).astype(jnp.float32).sum(axis=0)


def joined_along(pieces, dim):
    pieces = jnp.moveaxis(pieces, 0, dim)
    dims = pieces.shape
    return pieces.reshape(*dims[:dim], dims[dim] * dims[dim + 1], *dims[dim + 2 :])


def gather_directly(value, axis, dim):
    return joined_along(sent_to_all(value, axis), dim)


def in_blocks(value, dim, size):
    before, after = (value.shape[:dim], value.shape[dim + 1 :])
    return jnp.moveaxis(value.reshape(*before, size, -1, *after), dim, 0)


def sum_at_owner(value, axis, dim):
    pieces = in_blocks(value, dim, lax.axis_size(axis))
    arrived = lax.all_to_all(pieces, axis, split_axis=0, concat_axis=0, tiled=True)
    return arrived.astype(jnp.float32).sum(axis=0)


def layer_norm(value_entries, gain):
    average = jnp.mean(value_entries, axis=-1, keepdims=True)
    centred = value_entries - average
    spread = jnp.mean(centred * centred, axis=-1, keepdims=True)
    return centred * lax.rsqrt(spread + norm_eps) * gain.astype(jnp.float32)


def atom_windows(atoms, atom_counts, w_atom):
    slot_count = atoms.shape[0]
    channels = atoms.shape[1]
    local_width = w_atom.shape[2]
    head_size = channels // AH
    local_heads = local_width // head_size
    tail_rows = (KWIN - QWIN) // 2
    head_rows = (KWIN + QWIN) // 2
    live_total = jnp.sum(atom_counts)
    device_pos = lax.axis_index("tok")
    device_last = lax.axis_size("tok") - 1
    tail_block = lax.dynamic_slice_in_dim(atoms, live_total - tail_rows, tail_rows, 0)
    previous = from_behind(tail_block, "tok", 1)
    following = from_behind(atoms[:head_rows], "tok", -1)
    extended = jnp.concatenate([atoms, jnp.zeros((head_rows, channels), atoms.dtype)], axis=0)
    extended = lax.dynamic_update_slice(extended, following, (live_total, jnp.int32(0)))
    keyed_rows = jnp.concatenate([previous, extended], axis=0)
    projected_rows = jnp.dot(
        keyed_rows, w_atom.reshape(channels, 3 * local_width), preferred_element_type=jnp.float32
    ).astype(jnp.bfloat16)
    windows = slot_count // QWIN
    queries = projected_rows[tail_rows : tail_rows + slot_count, :local_width].reshape(
        windows, QWIN, local_heads, head_size
    )
    blocked = projected_rows[:, local_width:].reshape(windows + KWIN // QWIN, QWIN, 2 * local_width)
    stacked = jnp.stack(
        [blocked[step_pos : step_pos + windows] for step_pos in range(KWIN // QWIN)], axis=1
    )
    stacked = stacked.reshape(windows, KWIN, 2, local_heads, head_size)
    key_rows = stacked[:, :, 0]
    value_rows = stacked[:, :, 1]
    scores = jnp.einsum(
        "wqhd,wkhd->whqk", queries, key_rows, preferred_element_type=jnp.float32
    ) * head_size ** (-0.5)
    window_pos = jnp.arange(windows, dtype=jnp.int32)
    key_pos = window_pos[:, None] * QWIN + jnp.arange(KWIN, dtype=jnp.int32)[None, :] - tail_rows
    key_valid = (
        (key_pos < 0) & (device_pos > 0)
        | (key_pos >= 0) & (key_pos < live_total)
        | (key_pos >= live_total) & (device_pos < device_last)
    )
    scores = jnp.where(key_valid[:, None, None, :], scores, masked_value)
    row_max = jnp.max(scores, axis=-1, keepdims=True)
    lifted = jnp.exp(scores - row_max)
    weights = (lifted / jnp.sum(lifted, axis=-1, keepdims=True)).astype(jnp.bfloat16)
    atom_out = jnp.einsum(
        "whqk,wkhd->wqhd", weights, value_rows, preferred_element_type=jnp.float32
    )
    query_live = (jnp.arange(slot_count, dtype=jnp.int32) < live_total).reshape(windows, QWIN)
    atom_out = jnp.where(query_live[:, :, None, None], atom_out, 0.0)
    return atom_out.reshape(slot_count, local_width).astype(jnp.bfloat16)


def token_means(atom_out, atom_counts):
    starts = jnp.cumsum(atom_counts) - atom_counts
    slot_position = jnp.arange(atom_out.shape[0], dtype=jnp.int32)
    member = (slot_position[None, :] >= starts[:, None]) & (
        slot_position[None, :] < (starts + atom_counts)[:, None]
    )
    totals_rows = jnp.dot(member.astype(jnp.bfloat16), atom_out, preferred_element_type=jnp.float32)
    return totals_rows / atom_counts[:, None].astype(jnp.float32)


def shards(
    single,
    pair,
    atoms,
    atom_counts,
    w_atom,
    w_atom_token,
    ln_gain,
    w_proj,
    w_pair_bias,
    w_out,
    ln_gain2,
    w_trans,
    w_trans_out,
):
    atom_out = atom_windows(atoms, atom_counts, w_atom)
    token_atoms = token_means(atom_out, atom_counts).astype(jnp.bfloat16)
    atom_part = jnp.dot(token_atoms, w_atom_token, preferred_element_type=jnp.float32)
    atom_term = of_everyone(atom_part.astype(jnp.bfloat16), "head").astype(jnp.float32)
    residual_state = single.astype(jnp.float32) + atom_term
    normed = layer_norm(residual_state, ln_gain).astype(jnp.bfloat16)
    model_width = single.shape[1]
    local_width = w_proj.shape[2]
    head_size = model_width // H
    local_heads = local_width // head_size
    row_count = normed.shape[0]
    flat_proj = w_proj.reshape(model_width, 4 * local_width)
    own_proj = jnp.dot(normed, flat_proj, preferred_element_type=jnp.float32)
    queries = own_proj[:, :local_width].astype(jnp.bfloat16)
    gate_raw = own_proj[:, 3 * local_width :]
    key_value = own_proj[:, local_width : 3 * local_width].astype(jnp.bfloat16)
    gathered = gather_directly(key_value, "tok", 0)
    token_count = gathered.shape[0]
    key_value_rows = gathered.reshape(token_count, 2, local_heads, head_size)
    pair_term = jnp.einsum(
        "ikc,ch->hik", pair, w_pair_bias, preferred_element_type=jnp.float32
    ).astype(jnp.bfloat16)
    pair_term = lax.all_to_all(pair_term, "head", split_axis=0, concat_axis=2, tiled=True)
    query_rows = queries.reshape(row_count, local_heads, head_size)
    scores = jnp.einsum(
        "qhd,khd->hqk", query_rows, key_value_rows[:, 0], preferred_element_type=jnp.float32
    ) * head_size ** (-0.5)
    scores = scores + pair_term.astype(jnp.float32)
    row_max = jnp.max(scores, axis=-1, keepdims=True)
    lifted = jnp.exp(scores - row_max)
    weights = (lifted / jnp.sum(lifted, axis=-1, keepdims=True)).astype(jnp.bfloat16)
    context = jnp.einsum(
        "hqk,khd->qhd", weights, key_value_rows[:, 1], preferred_element_type=jnp.float32
    )
    context = context.reshape(row_count, local_width)
    gated_rows = (context * jax.nn.sigmoid(gate_raw)).astype(jnp.bfloat16)
    mixing = jnp.dot(gated_rows, w_out, preferred_element_type=jnp.float32)
    quarter = model_width // lax.axis_size("head")
    offset = lax.axis_index("head") * quarter
    state_after = residual_state + of_everyone(mixing.astype(jnp.bfloat16), "head").astype(
        jnp.float32
    )
    own_share = lax.dynamic_slice_in_dim(state_after, offset, quarter, 1)
    normed_after = layer_norm(state_after, ln_gain2).astype(jnp.bfloat16)
    hidden_local = w_trans.shape[2]
    gate_up = jnp.dot(
        normed_after,
        w_trans.reshape(model_width, 2 * hidden_local),
        preferred_element_type=jnp.float32,
    )
    hidden = (jax.nn.silu(gate_up[:, :hidden_local]) * gate_up[:, hidden_local:]).astype(
        jnp.bfloat16
    )
    update = sum_at_owner(
        jnp.dot(hidden, w_trans_out, preferred_element_type=jnp.float32).astype(jnp.bfloat16),
        "head",
        1,
    )
    refined = (own_share + update).astype(jnp.bfloat16)
    return (refined, atom_out.T)


def solution(mesh):
    return jax.shard_map(
        shards,
        mesh=mesh,
        in_specs=(
            P("tok", None),
            P("tok", "head", None),
            P("tok", None),
            P("tok"),
            P(None, None, "head"),
            P("head", None),
            P(),
            P(None, None, "head"),
            P(),
            P("head", None),
            P(),
            P(None, None, "head"),
            P("head", None),
        ),
        out_specs=(P("tok", "head"), P("head", "tok")),
        check_vma=False,
    )
```

profile of v0, /device:TPU:2, one launch (start us, length us, event | category | flops | bytes accessed | tf_op | source)
XLA Modules:
  0.0 143.4 jit_solution(10837507547731607174)
XLA Ops:
  0.6 0.8 copy.53
  1.6 1.9 %fusion.67 = (f32[32]{0:T(128)S(1)}, s32[32]{0:T(128)}, s32[]{:T(128)}) fusion(s32[32]{0:T(128)} %param.16, s32[32]{0:T(128)S(1)} %reduce.4), kind=kLoop, calls=%fused_computation.98 | loop fusion | flops 95 | bytes 516 | tf_op jit(solution)/shard_map/convert_element_type | solution.py:117
  4.8 0.7 constant_dynamic-slice_fusion
  5.6 1.9 %collective-permute-start = (bf16[48,128]{1,0:T(8,128)(2,1)S(1)}, bf16[48,128]{1,0:T(8,128)(2,1)S(1)}, u32[]{:S(2)}, u32[]{:S(2)}) collective-permute-start(bf16[48,128]{1,0:T(8,128)(2,1)S(1)} %constant_dynamic-slice_fusion), channel_id=1, source_target_pairs={{0,4},{4,8},{8,12},{12,16},{16,20},{20,24},{24,28},{28,32},{32,36}... | collective-permute-start | bytes 36872 | tf_op jit(solution)/shard_map/ppermute | solution.py:17
  7.5 0.7 slice.56
  8.2 3.6 %collective-permute-start.1 = (bf16[80,128]{1,0:T(8,128)(2,1)S(1)}, bf16[80,128]{1,0:T(8,128)(2,1)S(1)}, u32[]{:S(2)}, u32[]{:S(2)}) collective-permute-start(bf16[80,128]{1,0:T(8,128)(2,1)S(1)} %slice.56), channel_id=1, source_target_pairs={{4,0},{8,4},{12,8},{16,12},{20,16},{24,20},{28,24},{32,28},{36,32}... | collective-permute-start | bytes 61448 | tf_op jit(solution)/shard_map/ppermute | solution.py:17
  11.9 0.7 fusion.51
  12.6 0.7 add_compare_fusion
  14.5 0.9 concatenate.6
  16.2 0.2 dynamic_update_slice.3
  16.4 1.0 convolution_convert_fusion.1
  17.4 0.2 fusion.66
  17.5 0.7 slice.76
  18.2 0.2 copy.54
  18.4 0.2 copy.55
  18.6 0.2 copy.56
  18.7 0.2 copy.57
  18.9 0.2 pad_maximum_fusion
  19.1 1.0 copy.58
  20.2 0.8 reshape.173
  21.0 0.2 copy.70
  21.2 0.2 fusion.7
  21.4 0.3 fusion.68
  21.7 1.4 fusion.10
  23.2 0.1 convert_element_type.91
  23.4 0.3 convolution_convert_fusion.3
  23.7 0.7 broadcast_in_dim.34
  24.4 4.5 %all-to-all-start = ((bf16[4,32,768]{2,1,0:T(8,128)(2,1)}), bf16[4,32,768]{2,1,0:T(8,128)(2,1)S(1)}, u32[]{:S(2)}, u32[]{:S(2)}) async-start(bf16[4,32,768]{2,1,0:T(8,128)(2,1)} %broadcast_in_dim.34), calls=%async_computation | async-start | bytes 393216 | tf_op jit(solution)/shard_map/all_to_all | solution.py:22
  28.9 3.4 %convolution_convert_fusion = bf16[16,32,512]{2,0,1:T(8,128)(2,1)S(1)} fusion(bf16[32,512,128]{2,1,0:T(8,128)(2,1)} %param.14, bf16[128,16]{0,1:T(8,128)(2,1)S(1)} %copy-done.8), kind=kOutput, calls=%fused_computation.6 | convolution fusion | flops 67371008 | bytes 4722688 | tf_op jit(solution)/shard_map/ikc,ch->hik/dot_general | solution.py:154
  32.3 1.1 copy.66
  33.4 1.8 %all-to-all-done = bf16[4,32,768]{2,1,0:T(8,128)(2,1)S(1)} async-done(((bf16[4,32,768]{2,1,0:T(8,128)(2,1)}), bf16[4,32,768]{2,1,0:T(8,128)(2,1)S(1)}, u32[]{:S(2)}, u32[]{:S(2)}) %all-to-all-start) | async-done | bytes 196640 | tf_op jit(solution)/shard_map/all_to_all | solution.py:22
  35.2 3.5 %all-to-all-start.2 = ((bf16[16,32,512]{2,1,0:T(8,128)(2,1)}), bf16[16,32,512]{2,1,0:T(8,128)(2,1)S(1)}, u32[]{:S(2)}, u32[]{:S(2)}) async-start(bf16[16,32,512]{2,1,0:T(8,128)(2,1)} %copy.66), calls=%async_computation.2 | async-start | bytes 1048576 | tf_op jit(solution)/shard_map/all_to_all | solution.py:157
  38.8 0.2 multiply_reduce_fusion.1
  39.1 0.5 fusion.69
  39.5 0.6 copy-done.6
  40.3 6.9 %all-to-all-done.2 = bf16[16,32,512]{2,1,0:T(8,128)(2,1)S(1)} async-done(((bf16[16,32,512]{2,1,0:T(8,128)(2,1)}), bf16[16,32,512]{2,1,0:T(8,128)(2,1)S(1)}, u32[]{:S(2)}, u32[]{:S(2)}) %all-to-all-start.2) | async-done | bytes 524320 | tf_op jit(solution)/shard_map/all_to_all | solution.py:157
  47.2 1.3 broadcast_in_dim.35
  48.4 12.4 %all-to-all-start.1 = ((bf16[64,32,384]{2,1,0:T(8,128)(2,1)}), bf16[64,32,384]{2,1,0:T(8,128)(2,1)S(1)}, u32[]{:S(2)}, u32[]{:S(2)}) async-start(bf16[64,32,384]{2,1,0:T(8,128)(2,1)} %broadcast_in_dim.35), calls=%async_computation.1 | async-start | bytes 3145728 | tf_op jit(solution)/shard_map/all_to_all | solution.py:22
  60.9 1.3 slice.80
  62.2 0.8 reshape.178
  63.0 1.4 copy.80
  64.4 2.9 %reshape.182 = f32[4,32,2048]{2,1,0:T(8,128)} reshape(f32[4,32,4,512]{3,2,1,0:T(4,128)} %bitcast.71) | data formatting | bytes 2097152 | tf_op jit(solution)/shard_map/convert_element_type | solution.py:162
  67.3 33.6 %all-to-all-done.1 = bf16[64,32,384]{2,1,0:T(8,128)(2,1)S(1)} async-done(((bf16[64,32,384]{2,1,0:T(8,128)(2,1)}), bf16[64,32,384]{2,1,0:T(8,128)(2,1)S(1)}, u32[]{:S(2)}, u32[]{:S(2)}) %all-to-all-start.1) | async-done | bytes 1572896 | tf_op jit(solution)/shard_map/all_to_all | solution.py:22
  100.9 4.7 %reshape_reshape.3 = bf16[2048,2,4,48]{3,2,1,0:T(4,128)(2,1)} reshape(bf16[64,32,384]{2,1,0:T(8,128)(2,1)S(1)} %all-to-all-done.1) | data formatting | bytes 3145728 | tf_op jit(solution)/shard_map/reshape;reshape | solution.py:153
  105.6 4.0 %fusion.65 = (bf16[2048,1,4,48]{3,2,1,0:T(4,128)(2,1)}, bf16[2048,1,4,48]{3,2,1,0:T(4,128)(2,1)S(1)}) fusion(bf16[2048,2,4,48]{3,2,1,0:T(4,128)(2,1)} %reshape_reshape.3), kind=kLoop, calls=%fused_computation.96 | loop fusion | bytes 3145728 | tf_op jit(solution)/shard_map/slice | solution.py:160
  109.6 4.0 %copy.74 = bf16[2048,1,4,48]{0,3,2,1:T(8,128)(2,1)} copy(bf16[2048,1,4,48]{3,2,1,0:T(4,128)(2,1)} %get-tuple-element.4) | data formatting | bytes 1572864
  113.6 1.7 %fusion.4 = f32[4,32,2048]{2,1,0:T(8,128)S(1)} fusion(f32[4,32,2048]{2,1,0:T(8,128)} %reshape.182, bf16[2048,1,4,48]{0,3,2,1:T(8,128)(2,1)} %copy.74, bf16[32,4,48]{2,1,0:T(4,128)(2,1)S(1)} %reshape.178), kind=kOutput, calls=%fused_computation.5 | convolution fusion | flops 25690112 | bytes 2895872 | tf_op jit(solution)/shard_map/qhd,khd->hqk/dot_general | solution.py:159
  115.4 1.0 copy-done.1
  116.4 0.3 fusion.70
  116.7 2.3 %copy.73 = bf16[2048,1,4,48]{0,3,2,1:T(8,128)(2,1)} copy(bf16[2048,1,4,48]{3,2,1,0:T(4,128)(2,1)S(1)} %get-tuple-element.5) | data formatting | bytes 1572864
  119.1 2.2 %convolution_bitcast_fusion.1 = f32[32,4,48]{2,0,1:T(8,128)S(1)} fusion(bf16[2048,1,4,48]{0,3,2,1:T(8,128)(2,1)} %copy.73, f32[4,32]{1,0:T(4,128)S(1)} %fusion.70, f32[4,32,2048]{2,1,0:T(8,128)} %copy-done.1), kind=kOutput, calls=%fused_computation.19 | convolution fusion | flops 25954432 | bytes 1860096 | tf_op jit(solution)/shard_map/hqk,khd->qhd/dot_general | solution.py:166
  121.5 0.2 convolution_convert_fusion.2
  121.7 0.7 broadcast_in_dim.36
  122.4 3.4 %all-to-all-start.3 = ((bf16[4,32,768]{2,1,0:T(8,128)(2,1)}), bf16[4,32,768]{2,1,0:T(8,128)(2,1)S(1)}, u32[]{:S(2)}, u32[]{:S(2)}) async-start(bf16[4,32,768]{2,1,0:T(8,128)(2,1)} %broadcast_in_dim.36), calls=%async_computation.3 | async-start | bytes 393216 | tf_op jit(solution)/shard_map/all_to_all | solution.py:22
  125.8 1.5 %copy.75 = bf16[96,8,2,384]{3,1,2,0:T(8,128)(2,1)S(1)} copy(bf16[96,8,2,384]{3,2,1,0:T(2,128)(2,1)} %bitcast.73) | data formatting | bytes 2359296
  127.3 4.8 %all-to-all-done.3 = bf16[4,32,768]{2,1,0:T(8,128)(2,1)S(1)} async-done(((bf16[4,32,768]{2,1,0:T(8,128)(2,1)}), bf16[4,32,768]{2,1,0:T(8,128)(2,1)S(1)}, u32[]{:S(2)}, u32[]{:S(2)}) %all-to-all-start.3) | async-done | bytes 196640 | tf_op jit(solution)/shard_map/all_to_all | solution.py:22
  132.1 0.1 fusion.63
  132.2 0.2 multiply_reduce_fusion
  132.4 0.4 fusion.23
  132.8 0.2 convolution_convert_fusion.4
  133.1 0.6 copy.81
  133.8 3.3 %all-to-all-start.4 = ((bf16[4,32,192]{2,1,0:T(8,128)(2,1)}), bf16[4,32,192]{2,1,0:T(8,128)(2,1)S(1)}, u32[]{:S(2)}, u32[]{:S(2)}) async-start(bf16[4,32,192]{2,1,0:T(8,128)(2,1)} %bitcast.68), calls=%async_computation.4 | async-start | bytes 131072 | tf_op jit(solution)/shard_map/all_to_all | solution.py:46
  137.1 5.6 %all-to-all-done.4 = bf16[4,32,192]{2,1,0:T(8,128)(2,1)S(1)} async-done(((bf16[4,32,192]{2,1,0:T(8,128)(2,1)}), bf16[4,32,192]{2,1,0:T(8,128)(2,1)S(1)}, u32[]{:S(2)}, u32[]{:S(2)}) %all-to-all-start.4) | async-done | bytes 49184 | tf_op jit(solution)/shard_map/all_to_all | solution.py:46
  142.7 0.7 add_convert_fusion
  (44 shorter events, 0.9 us)
Async XLA Ops:
  0.6 38.4 %copy-start = (bf16[768,4,192]{0,2,1:T(8,128)(2,1)S(1)}, bf16[768,4,192]{0,2,1:T(8,128)(2,1)}, u32[]{:S(2)}) copy-start(bf16[768,4,192]{0,2,1:T(8,128)(2,1)} %param.20) | copy-start | bytes 3538948
  5.6 10.9 %collective-permute-start = (bf16[48,128]{1,0:T(8,128)(2,1)S(1)}, bf16[48,128]{1,0:T(8,128)(2,1)S(1)}, u32[]{:S(2)}, u32[]{:S(2)}) collective-permute-start(bf16[48,128]{1,0:T(8,128)(2,1)S(1)} %constant_dynamic-slice_fusion), channel_id=1, source_target_pairs={{0,4},{4,8},{8,12},{12,16},{16,20},{20,24},{24,28},{28,32},{32,36}... | collective-permute-start | bytes 36872 | tf_op jit(solution)/shard_map/ppermute | solution.py:17
  8.2 7.9 %collective-permute-start.1 = (bf16[80,128]{1,0:T(8,128)(2,1)S(1)}, bf16[80,128]{1,0:T(8,128)(2,1)S(1)}, u32[]{:S(2)}, u32[]{:S(2)}) collective-permute-start(bf16[80,128]{1,0:T(8,128)(2,1)S(1)} %slice.56), channel_id=1, source_target_pairs={{4,0},{8,4},{12,8},{16,12},{20,16},{24,20},{28,24},{32,28},{36,32}... | collective-permute-start | bytes 61448 | tf_op jit(solution)/shard_map/ppermute | solution.py:17
  20.2 0.8 copy-start.5
  21.4 2.0 %copy-start.11 = (s32[32]{0:T(128)S(1)}, s32[32]{0:T(128)}, u32[]{:S(2)}) copy-start(s32[32]{0:T(128)} %get-tuple-element.11) | copy-start | bytes 388
  21.4 2.0 %copy-start.12 = (bf16[32,768]{1,0:T(8,128)(2,1)S(1)}, bf16[32,768]{1,0:T(8,128)(2,1)}, u32[]{:S(2)}) copy-start(bf16[32,768]{1,0:T(8,128)(2,1)} %param.18) | copy-start | bytes 147460
  21.7 7.2 %copy-start.8 = (bf16[128,16]{0,1:T(8,128)(2,1)S(1)}, bf16[128,16]{0,1:T(8,128)(2,1)}, u32[]{:S(2)}) copy-start(bf16[128,16]{0,1:T(8,128)(2,1)} %param.21) | copy-start | bytes 12292
  23.3 8.9 %copy-start.7 = (bf16[768,32]{0,1:T(8,128)(2,1)}, bf16[768,32]{0,1:T(8,128)(2,1)S(1)}, u32[]{:S(2)}) copy-start(bf16[768,32]{0,1:T(8,128)(2,1)S(1)} %convert_element_type.91) | copy-start | bytes 147460
  24.4 10.8 %all-to-all-start = ((bf16[4,32,768]{2,1,0:T(8,128)(2,1)}), bf16[4,32,768]{2,1,0:T(8,128)(2,1)S(1)}, u32[]{:S(2)}, u32[]{:S(2)}) async-start(bf16[4,32,768]{2,1,0:T(8,128)(2,1)} %broadcast_in_dim.34), calls=%async_computation | async-start | bytes 393216 | tf_op jit(solution)/shard_map/all_to_all | solution.py:22
  28.9 3.4 %copy-start.9 = (bf16[768]{0:T(1024)(128)(2,1)S(1)}, bf16[768]{0:T(1024)(128)(2,1)}, u32[]{:S(2)}) copy-start(bf16[768]{0:T(1024)(128)(2,1)} %param.19) | copy-start | bytes 4612
  32.3 6.4 %copy-start.2 = (bf16[32,768]{1,0:T(8,128)(2,1)S(1)}, bf16[32,768]{1,0:T(8,128)(2,1)}, u32[]{:S(2)}) copy-start(bf16[32,768]{1,0:T(8,128)(2,1)} %param.13) | copy-start | bytes 147460
  35.2 12.0 %all-to-all-start.2 = ((bf16[16,32,512]{2,1,0:T(8,128)(2,1)}), bf16[16,32,512]{2,1,0:T(8,128)(2,1)S(1)}, u32[]{:S(2)}, u32[]{:S(2)}) async-start(bf16[16,32,512]{2,1,0:T(8,128)(2,1)} %copy.66), calls=%async_computation.2 | async-start | bytes 1048576 | tf_op jit(solution)/shard_map/all_to_all | solution.py:157
  39.5 0.6 copy-start.6
  48.4 52.5 %all-to-all-start.1 = ((bf16[64,32,384]{2,1,0:T(8,128)(2,1)}), bf16[64,32,384]{2,1,0:T(8,128)(2,1)S(1)}, u32[]{:S(2)}, u32[]{:S(2)}) async-start(bf16[64,32,384]{2,1,0:T(8,128)(2,1)} %broadcast_in_dim.35), calls=%async_computation.1 | async-start | bytes 3145728 | tf_op jit(solution)/shard_map/all_to_all | solution.py:22
  115.4 1.0 copy-start.1
  119.1 2.4 %copy-start.4 = (bf16[192,768]{1,0:T(8,128)(2,1)S(1)}, bf16[192,768]{1,0:T(8,128)(2,1)}, u32[]{:S(2)}) copy-start(bf16[192,768]{1,0:T(8,128)(2,1)} %param.22) | copy-start | bytes 884740
  121.7 5.6 %copy-start.10 = (bf16[768]{0:T(1024)(128)(2,1)S(1)}, bf16[768]{0:T(1024)(128)(2,1)}, u32[]{:S(2)}) copy-start(bf16[768]{0:T(1024)(128)(2,1)} %param.23) | copy-start | bytes 4612
  122.4 9.7 %all-to-all-start.3 = ((bf16[4,32,768]{2,1,0:T(8,128)(2,1)}), bf16[4,32,768]{2,1,0:T(8,128)(2,1)S(1)}, u32[]{:S(2)}, u32[]{:S(2)}) async-start(bf16[4,32,768]{2,1,0:T(8,128)(2,1)} %broadcast_in_dim.36), calls=%async_computation.3 | async-start | bytes 393216 | tf_op jit(solution)/shard_map/all_to_all | solution.py:22
  127.3 5.5 %copy-start.3 = (bf16[384,768]{1,0:T(8,128)(2,1)S(1)}, bf16[384,768]{1,0:T(8,128)(2,1)}, u32[]{:S(2)}) copy-start(bf16[384,768]{1,0:T(8,128)(2,1)} %param.25) | copy-start | bytes 1769476
  133.8 8.9 %all-to-all-start.4 = ((bf16[4,32,192]{2,1,0:T(8,128)(2,1)}), bf16[4,32,192]{2,1,0:T(8,128)(2,1)S(1)}, u32[]{:S(2)}, u32[]{:S(2)}) async-start(bf16[4,32,192]{2,1,0:T(8,128)(2,1)} %bitcast.68), calls=%async_computation.4 | async-start | bytes 131072 | tf_op jit(solution)/shard_map/all_to_all | solution.py:46
where the time goes:
time: 145 us; the launch traced here: 143 us
  waiting for transfers between devices  52.6 us (36%)
  local copies, waits for them, and re-layouts  36.7 us (25%)
  starting transfers between devices  32.6 us (22%)
  matrix products  11.5 us (8%)
  other arithmetic  5.67 us (4%)
  between operations  4.3 us (3%)
    all_to_all x3, waiting for transfers between devices, sent_to_all(): return lax.all_to_all(copies, axis, split_axis=0, concat_axis=0, tiled=True)  40.1 us
    all_to_all x3, starting transfers between devices, sent_to_all(): return lax.all_to_all(copies, axis, split_axis=0, concat_axis=0, tiled=True)  20.3 us
    unnamed x29, local copies, waits for them, and re-layouts  9.59 us
    all_to_all x1, waiting for transfers between devices, shards(): lax.all_to_all(pair_term, 'head', split_axis=0, concat_axis=2, tiled=True)  6.9 us
    all_to_all x1, waiting for transfers between devices, sum_at_owner(): lax.all_to_all(pieces, axis, split_axis=0, concat_axis=0, tiled=True)  5.58 us
    ppermute x2, starting transfers between devices, from_behind(): return lax.ppermute(block, axis, route)  5.54 us
    another operation x1, local copies, waits for them, and re-layouts, shards(): key_value_rows = gathered.reshape(token_count, 2, local_heads, head_size)  4.66 us
    convert_element_type x2, local copies, waits for them, and re-layouts, shards(): scores = scores + pair_term.astype(jnp.float32)  4.32 us
  transfers between devices with their start and end apart: 7, of which 5 were waited for; matrix products, arithmetic and copies ran while one was open for 12% of the time, Pallas kernels for 0%

commit v1 on v0

--- a/solution.py
+++ b/solution.py
@@ -154,7 +154,12 @@
     pair_term = jnp.einsum(
         "ikc,ch->hik", pair, w_pair_bias, preferred_element_type=jnp.float32
     ).astype(jnp.bfloat16)
-    pair_term = lax.all_to_all(pair_term, "head", split_axis=0, concat_axis=2, tiled=True)
+    pair_term = jnp.concatenate(
+        lax.all_to_all(
+            jnp.stack(jnp.split(pair_term, lax.axis_size("head"), axis=0)), "head", 0, 0
+        ),
+        axis=2,
+    )
     query_rows = queries.reshape(row_count, local_heads, head_size)
     scores = jnp.einsum(
         "qhd,khd->hqk", query_rows, key_value_rows[:, 0], preferred_element_type=jnp.float32

time: 145 us -> 147 us (1.014)
  waiting for transfers between devices: 52.6 us -> 55.1 us
  local copies, waits for them, and re-layouts: 36.7 us -> 35.1 us
    all_to_all x3, waiting for transfers between devices: 40.1 us -> 42.8 us  [sent_to_all(): return lax.all_to_all(copies, axis, split_axis=0, concat_axis=0, tiled=True)]
    unnamed x29 -> x33, local copies, waits for them, and re-layouts: 9.59 us -> 9.58 us
where the time goes in v1:
time: 147 us; the launch traced here: 146 us
  waiting for transfers between devices  55.1 us (37%)
  local copies, waits for them, and re-layouts  35.1 us (24%)
  starting transfers between devices  32.7 us (22%)
  matrix products  11.6 us (8%)
  other arithmetic  7.07 us (5%)
  between operations  4.34 us (3%)
    all_to_all x3, waiting for transfers between devices, sent_to_all(): return lax.all_to_all(copies, axis, split_axis=0, concat_axis=0, tiled=True)  42.8 us
    all_to_all x3, starting transfers between devices, sent_to_all(): return lax.all_to_all(copies, axis, split_axis=0, concat_axis=0, tiled=True)  20.4 us
    unnamed x33, local copies, waits for them, and re-layouts  9.58 us
    all_to_all x1, waiting for transfers between devices, shards(): lax.all_to_all(jnp.stack(jnp.split(pair_term, lax.axis_size('head'), axis...  6.75 us
    all_to_all x1, waiting for transfers between devices, sum_at_owner(): lax.all_to_all(pieces, axis, split_axis=0, concat_axis=0, tiled=True)  5.58 us
    ppermute x2, starting transfers between devices, from_behind(): return lax.ppermute(block, axis, route)  5.54 us
    another operation x1, local copies, waits for them, and re-layouts, shards(): key_value_rows = gathered.reshape(token_count, 2, local_heads, head_size)  4.66 us
    convert_element_type x2, local copies, waits for them, and re-layouts, shards(): scores = scores + pair_term.astype(jnp.float32)  4.59 us
  transfers between devices with their start and end apart: 7, of which 5 were waited for; matrix products, arithmetic and copies ran while one was open for 12% of the time, Pallas kernels for 0%

profile of v1, /device:TPU:2, one launch (start us, length us, event | category | flops | bytes accessed | tf_op | source)
XLA Modules:
  0.0 146.0 jit_solution(17943218632257808581)
XLA Ops:
  0.6 0.8 copy.52
  1.6 1.9 %fusion.67 = (f32[32]{0:T(128)S(1)}, s32[32]{0:T(128)}, s32[]{:T(128)}) fusion(s32[32]{0:T(128)} %param.16, s32[32]{0:T(128)S(1)} %reduce.4), kind=kLoop, calls=%fused_computation.103 | loop fusion | flops 95 | bytes 516 | tf_op jit(solution)/shard_map/convert_element_type | solution.py:117
  4.8 0.7 constant_dynamic-slice_fusion
  5.6 1.9 %collective-permute-start = (bf16[48,128]{1,0:T(8,128)(2,1)S(1)}, bf16[48,128]{1,0:T(8,128)(2,1)S(1)}, u32[]{:S(2)}, u32[]{:S(2)}) collective-permute-start(bf16[48,128]{1,0:T(8,128)(2,1)S(1)} %constant_dynamic-slice_fusion), channel_id=1, source_target_pairs={{0,4},{4,8},{8,12},{12,16},{16,20},{20,24},{24,28},{28,32},{32,36}... | collective-permute-start | bytes 36872 | tf_op jit(solution)/shard_map/ppermute | solution.py:17
  7.5 0.7 slice.56
  8.2 3.6 %collective-permute-start.1 = (bf16[80,128]{1,0:T(8,128)(2,1)S(1)}, bf16[80,128]{1,0:T(8,128)(2,1)S(1)}, u32[]{:S(2)}, u32[]{:S(2)}) collective-permute-start(bf16[80,128]{1,0:T(8,128)(2,1)S(1)} %slice.56), channel_id=1, source_target_pairs={{4,0},{8,4},{12,8},{16,12},{20,16},{24,20},{28,24},{32,28},{36,32}... | collective-permute-start | bytes 61448 | tf_op jit(solution)/shard_map/ppermute | solution.py:17
  11.9 4.2 %convolution_convert_fusion = bf16[16,32,512]{2,0,1:T(8,128)(2,1)} fusion(bf16[32,512,128]{2,1,0:T(8,128)(2,1)} %param.14, bf16[128,16]{0,1:T(8,128)(2,1)} %param.21), kind=kOutput, calls=%fused_computation.6 | convolution fusion | flops 67371008 | bytes 4722688 | tf_op jit(solution)/shard_map/ikc,ch->hik/dot_general | solution.py:154
  16.1 0.7 fusion.51
  16.9 0.7 add_compare_fusion
  19.5 0.2 dynamic_update_slice.3
  19.8 0.2 convolution_convert_fusion.1
  20.0 0.2 fusion.66
  20.2 0.7 slice.76
  20.9 0.2 copy.53
  21.0 0.2 copy.54
  21.2 0.2 copy.55
  21.4 0.2 copy.56
  21.5 0.2 pad_maximum_fusion
  21.8 1.0 copy.57
  22.8 0.8 reshape.173
  23.6 0.2 copy.68
  23.8 0.2 fusion.7
  24.0 0.3 fusion.68
  24.3 1.4 fusion.10
  25.8 0.1 convert_element_type.88
  26.0 0.3 convolution_convert_fusion.3
  26.3 0.7 broadcast_in_dim.34
  27.0 4.5 %all-to-all-start = ((bf16[4,32,768]{2,1,0:T(8,128)(2,1)}), bf16[4,32,768]{2,1,0:T(8,128)(2,1)S(1)}, u32[]{:S(2)}, u32[]{:S(2)}) async-start(bf16[4,32,768]{2,1,0:T(8,128)(2,1)} %broadcast_in_dim.34), calls=%async_computation | async-start | bytes 393216 | tf_op jit(solution)/shard_map/all_to_all | solution.py:22
  31.5 0.2 slice_bitcast_fusion.7
  31.7 1.3 pad_maximum_fusion.1
  33.0 4.9 %all-to-all-done = bf16[4,32,768]{2,1,0:T(8,128)(2,1)S(1)} async-done(((bf16[4,32,768]{2,1,0:T(8,128)(2,1)}), bf16[4,32,768]{2,1,0:T(8,128)(2,1)S(1)}, u32[]{:S(2)}, u32[]{:S(2)}) %all-to-all-start) | async-done | bytes 196640 | tf_op jit(solution)/shard_map/all_to_all | solution.py:22
  37.8 3.5 %all-to-all-start.2 = ((bf16[4,4,32,512]{3,1,2,0:T(4,128)(2,1)}), bf16[4,4,32,512]{3,1,2,0:T(4,128)(2,1)S(1)}, u32[]{:S(2)}, u32[]{:S(2)}) async-start(bf16[4,4,32,512]{3,1,2,0:T(4,128)(2,1)} %pad_maximum_fusion.1), calls=%async_computation.2 | async-start | bytes 1048576 | tf_op jit(solution)/shard_map/all_to_all | solution.py:158
  41.5 0.2 multiply_reduce_fusion.1
  41.7 0.5 fusion.69
  42.2 0.6 copy-done.8
  42.9 6.8 %all-to-all-done.2 = bf16[4,4,32,512]{3,1,2,0:T(4,128)(2,1)S(1)} async-done(((bf16[4,4,32,512]{3,1,2,0:T(4,128)(2,1)}), bf16[4,4,32,512]{3,1,2,0:T(4,128)(2,1)S(1)}, u32[]{:S(2)}, u32[]{:S(2)}) %all-to-all-start.2) | async-done | bytes 524320 | tf_op jit(solution)/shard_map/all_to_all | solution.py:158
  49.6 1.3 broadcast_in_dim.35
  50.9 12.6 %all-to-all-start.1 = ((bf16[64,32,384]{2,1,0:T(8,128)(2,1)}), bf16[64,32,384]{2,1,0:T(8,128)(2,1)S(1)}, u32[]{:S(2)}, u32[]{:S(2)}) async-start(bf16[64,32,384]{2,1,0:T(8,128)(2,1)} %broadcast_in_dim.35), calls=%async_computation.1 | async-start | bytes 3145728 | tf_op jit(solution)/shard_map/all_to_all | solution.py:22
  63.5 1.3 slice.80
  64.8 0.8 reshape.178
  65.6 0.1 convert_bitcast_fusion
  65.8 1.6 %copy.65 = f32[4,32,4,512]{3,2,1,0:T(4,128)} copy(f32[4,32,4,512]{3,0,1,2:T(4,128)S(1)} %convert_bitcast_fusion) | data formatting | bytes 2097152 | tf_op jit(solution)/shard_map/convert_element_type | solution.py:167
  67.4 2.9 %reshape.182 = f32[4,32,2048]{2,1,0:T(8,128)} reshape(f32[4,32,4,512]{3,2,1,0:T(4,128)} %copy.65) | data formatting | bytes 2097152 | tf_op jit(solution)/shard_map/convert_element_type | solution.py:167
  70.4 33.2 %all-to-all-done.1 = bf16[64,32,384]{2,1,0:T(8,128)(2,1)S(1)} async-done(((bf16[64,32,384]{2,1,0:T(8,128)(2,1)}), bf16[64,32,384]{2,1,0:T(8,128)(2,1)S(1)}, u32[]{:S(2)}, u32[]{:S(2)}) %all-to-all-start.1) | async-done | bytes 1572896 | tf_op jit(solution)/shard_map/all_to_all | solution.py:22
  103.5 4.7 %reshape_reshape.3 = bf16[2048,2,4,48]{3,2,1,0:T(4,128)(2,1)} reshape(bf16[64,32,384]{2,1,0:T(8,128)(2,1)S(1)} %all-to-all-done.1) | data formatting | bytes 3145728 | tf_op jit(solution)/shard_map/reshape;reshape | solution.py:153
  108.2 4.0 %fusion.65 = (bf16[2048,1,4,48]{3,2,1,0:T(4,128)(2,1)}, bf16[2048,1,4,48]{3,2,1,0:T(4,128)(2,1)S(1)}) fusion(bf16[2048,2,4,48]{3,2,1,0:T(4,128)(2,1)} %reshape_reshape.3), kind=kLoop, calls=%fused_computation.101 | loop fusion | bytes 3145728 | tf_op jit(solution)/shard_map/slice | solution.py:165
  112.2 4.0 %copy.72 = bf16[2048,1,4,48]{0,3,2,1:T(8,128)(2,1)} copy(bf16[2048,1,4,48]{3,2,1,0:T(4,128)(2,1)} %get-tuple-element.4) | data formatting | bytes 1572864
  116.3 1.7 %fusion.4 = f32[4,32,2048]{2,1,0:T(8,128)S(1)} fusion(f32[4,32,2048]{2,1,0:T(8,128)} %reshape.182, bf16[2048,1,4,48]{0,3,2,1:T(8,128)(2,1)} %copy.72, bf16[32,4,48]{2,1,0:T(4,128)(2,1)S(1)} %reshape.178), kind=kOutput, calls=%fused_computation.5 | convolution fusion | flops 25690112 | bytes 2895872 | tf_op jit(solution)/shard_map/qhd,khd->hqk/dot_general | solution.py:164
  118.0 1.0 copy-done.1
  119.0 0.3 fusion.70
  119.3 2.3 %copy.71 = bf16[2048,1,4,48]{0,3,2,1:T(8,128)(2,1)} copy(bf16[2048,1,4,48]{3,2,1,0:T(4,128)(2,1)S(1)} %get-tuple-element.5) | data formatting | bytes 1572864
  121.7 2.2 %convolution_bitcast_fusion.1 = f32[32,4,48]{2,0,1:T(8,128)S(1)} fusion(bf16[2048,1,4,48]{0,3,2,1:T(8,128)(2,1)} %copy.71, f32[4,32]{1,0:T(4,128)S(1)} %fusion.70, f32[4,32,2048]{2,1,0:T(8,128)} %copy-done.1), kind=kOutput, calls=%fused_computation.19 | convolution fusion | flops 25954432 | bytes 1860096 | tf_op jit(solution)/shard_map/hqk,khd->qhd/dot_general | solution.py:171
  124.1 0.2 convolution_convert_fusion.2
  124.3 0.7 broadcast_in_dim.36
  125.0 3.4 %all-to-all-start.3 = ((bf16[4,32,768]{2,1,0:T(8,128)(2,1)}), bf16[4,32,768]{2,1,0:T(8,128)(2,1)S(1)}, u32[]{:S(2)}, u32[]{:S(2)}) async-start(bf16[4,32,768]{2,1,0:T(8,128)(2,1)} %broadcast_in_dim.36), calls=%async_computation.3 | async-start | bytes 393216 | tf_op jit(solution)/shard_map/all_to_all | solution.py:22
  128.4 1.5 %copy.73 = bf16[96,8,2,384]{3,1,2,0:T(8,128)(2,1)S(1)} copy(bf16[96,8,2,384]{3,2,1,0:T(2,128)(2,1)} %bitcast.76) | data formatting | bytes 2359296
  129.9 4.8 %all-to-all-done.3 = bf16[4,32,768]{2,1,0:T(8,128)(2,1)S(1)} async-done(((bf16[4,32,768]{2,1,0:T(8,128)(2,1)}), bf16[4,32,768]{2,1,0:T(8,128)(2,1)S(1)}, u32[]{:S(2)}, u32[]{:S(2)}) %all-to-all-start.3) | async-done | bytes 196640 | tf_op jit(solution)/shard_map/all_to_all | solution.py:22
  134.8 0.2 multiply_reduce_fusion
  135.0 0.4 fusion.23
  135.4 0.2 convolution_convert_fusion.4
  135.8 0.6 copy.77
  136.4 3.3 %all-to-all-start.4 = ((bf16[4,32,192]{2,1,0:T(8,128)(2,1)}), bf16[4,32,192]{2,1,0:T(8,128)(2,1)S(1)}, u32[]{:S(2)}, u32[]{:S(2)}) async-start(bf16[4,32,192]{2,1,0:T(8,128)(2,1)} %bitcast.73), calls=%async_computation.4 | async-start | bytes 131072 | tf_op jit(solution)/shard_map/all_to_all | solution.py:46
  139.7 5.6 %all-to-all-done.4 = bf16[4,32,192]{2,1,0:T(8,128)(2,1)S(1)} async-done(((bf16[4,32,192]{2,1,0:T(8,128)(2,1)}), bf16[4,32,192]{2,1,0:T(8,128)(2,1)S(1)}, u32[]{:S(2)}, u32[]{:S(2)}) %all-to-all-start.4) | async-done | bytes 49184 | tf_op jit(solution)/shard_map/all_to_all | solution.py:46
  145.3 0.7 add_convert_fusion
  (50 shorter events, 1.1 us)
Async XLA Ops:
  0.6 41.0 %copy-start = (bf16[768,4,192]{0,2,1:T(8,128)(2,1)S(1)}, bf16[768,4,192]{0,2,1:T(8,128)(2,1)}, u32[]{:S(2)}) copy-start(bf16[768,4,192]{0,2,1:T(8,128)(2,1)} %param.20) | copy-start | bytes 3538948
  5.6 14.2 %collective-permute-start = (bf16[48,128]{1,0:T(8,128)(2,1)S(1)}, bf16[48,128]{1,0:T(8,128)(2,1)S(1)}, u32[]{:S(2)}, u32[]{:S(2)}) collective-permute-start(bf16[48,128]{1,0:T(8,128)(2,1)S(1)} %constant_dynamic-slice_fusion), channel_id=1, source_target_pairs={{0,4},{4,8},{8,12},{12,16},{16,20},{20,24},{24,28},{28,32},{32,36}... | collective-permute-start | bytes 36872 | tf_op jit(solution)/shard_map/ppermute | solution.py:17
  8.2 11.3 %collective-permute-start.1 = (bf16[80,128]{1,0:T(8,128)(2,1)S(1)}, bf16[80,128]{1,0:T(8,128)(2,1)S(1)}, u32[]{:S(2)}, u32[]{:S(2)}) collective-permute-start(bf16[80,128]{1,0:T(8,128)(2,1)S(1)} %slice.56), channel_id=1, source_target_pairs={{4,0},{8,4},{12,8},{16,12},{20,16},{24,20},{28,24},{32,28},{36,32}... | collective-permute-start | bytes 61448 | tf_op jit(solution)/shard_map/ppermute | solution.py:17
  11.9 6.9 %copy-start.6 = (bf16[768,128]{1,0:T(8,128)(2,1)S(1)}, bf16[768,128]{1,0:T(8,128)(2,1)}, u32[]{:S(2)}) copy-start(bf16[768,128]{1,0:T(8,128)(2,1)} %param.15) | copy-start | bytes 589828
  11.9 7.9 %copy-start.14 = (bf16[128,3,32]{0,2,1:T(8,128)(2,1)S(1)}, bf16[128,3,32]{0,2,1:T(8,128)(2,1)}, u32[]{:S(2)}) copy-start(bf16[128,3,32]{0,2,1:T(8,128)(2,1)} %param.17) | copy-start | bytes 73732
  22.8 0.8 copy-start.7
  24.0 2.0 %copy-start.12 = (s32[32]{0:T(128)S(1)}, s32[32]{0:T(128)}, u32[]{:S(2)}) copy-start(s32[32]{0:T(128)} %get-tuple-element.15) | copy-start | bytes 388
  24.0 2.0 %copy-start.13 = (bf16[32,768]{1,0:T(8,128)(2,1)S(1)}, bf16[32,768]{1,0:T(8,128)(2,1)}, u32[]{:S(2)}) copy-start(bf16[32,768]{1,0:T(8,128)(2,1)} %param.18) | copy-start | bytes 147460
  24.3 7.2 %copy-start.2 = (bf16[16,32,512]{2,0,1:T(8,128)(2,1)S(1)}, bf16[16,32,512]{2,0,1:T(8,128)(2,1)}, u32[]{:S(2)}) copy-start(bf16[16,32,512]{2,0,1:T(8,128)(2,1)} %convolution_convert_fusion) | copy-start | bytes 1572868
  25.7 6.0 %copy-start.10 = (bf16[768]{0:T(1024)(128)(2,1)S(1)}, bf16[768]{0:T(1024)(128)(2,1)}, u32[]{:S(2)}) copy-start(bf16[768]{0:T(1024)(128)(2,1)} %param.19) | copy-start | bytes 4612
  26.0 1.1 copy-start.9
  27.0 10.8 %all-to-all-start = ((bf16[4,32,768]{2,1,0:T(8,128)(2,1)}), bf16[4,32,768]{2,1,0:T(8,128)(2,1)S(1)}, u32[]{:S(2)}, u32[]{:S(2)}) async-start(bf16[4,32,768]{2,1,0:T(8,128)(2,1)} %broadcast_in_dim.34), calls=%async_computation | async-start | bytes 393216 | tf_op jit(solution)/shard_map/all_to_all | solution.py:22
  31.5 9.8 %copy-start.3 = (bf16[32,768]{1,0:T(8,128)(2,1)S(1)}, bf16[32,768]{1,0:T(8,128)(2,1)}, u32[]{:S(2)}) copy-start(bf16[32,768]{1,0:T(8,128)(2,1)} %param.13) | copy-start | bytes 147460
  37.8 11.8 %all-to-all-start.2 = ((bf16[4,4,32,512]{3,1,2,0:T(4,128)(2,1)}), bf16[4,4,32,512]{3,1,2,0:T(4,128)(2,1)S(1)}, u32[]{:S(2)}, u32[]{:S(2)}) async-start(bf16[4,4,32,512]{3,1,2,0:T(4,128)(2,1)} %pad_maximum_fusion.1), calls=%async_computation.2 | async-start | bytes 1048576 | tf_op jit(solution)/shard_map/all_to_all | solution.py:158
  42.2 0.6 copy-start.8
  50.9 52.6 %all-to-all-start.1 = ((bf16[64,32,384]{2,1,0:T(8,128)(2,1)}), bf16[64,32,384]{2,1,0:T(8,128)(2,1)S(1)}, u32[]{:S(2)}, u32[]{:S(2)}) async-start(bf16[64,32,384]{2,1,0:T(8,128)(2,1)} %broadcast_in_dim.35), calls=%async_computation.1 | async-start | bytes 3145728 | tf_op jit(solution)/shard_map/all_to_all | solution.py:22
  118.0 1.0 copy-start.1
  121.7 2.4 %copy-start.5 = (bf16[192,768]{1,0:T(8,128)(2,1)S(1)}, bf16[192,768]{1,0:T(8,128)(2,1)}, u32[]{:S(2)}) copy-start(bf16[192,768]{1,0:T(8,128)(2,1)} %param.22) | copy-start | bytes 884740
  124.3 5.6 %copy-start.11 = (bf16[768]{0:T(1024)(128)(2,1)S(1)}, bf16[768]{0:T(1024)(128)(2,1)}, u32[]{:S(2)}) copy-start(bf16[768]{0:T(1024)(128)(2,1)} %param.23) | copy-start | bytes 4612
  125.0 9.7 %all-to-all-start.3 = ((bf16[4,32,768]{2,1,0:T(8,128)(2,1)}), bf16[4,32,768]{2,1,0:T(8,128)(2,1)S(1)}, u32[]{:S(2)}, u32[]{:S(2)}) async-start(bf16[4,32,768]{2,1,0:T(8,128)(2,1)} %broadcast_in_dim.36), calls=%async_computation.3 | async-start | bytes 393216 | tf_op jit(solution)/shard_map/all_to_all | solution.py:22
  129.9 5.5 %copy-start.4 = (bf16[384,768]{1,0:T(8,128)(2,1)S(1)}, bf16[384,768]{1,0:T(8,128)(2,1)}, u32[]{:S(2)}) copy-start(bf16[384,768]{1,0:T(8,128)(2,1)} %param.25) | copy-start | bytes 1769476
  136.4 8.9 %all-to-all-start.4 = ((bf16[4,32,192]{2,1,0:T(8,128)(2,1)}), bf16[4,32,192]{2,1,0:T(8,128)(2,1)S(1)}, u32[]{:S(2)}, u32[]{:S(2)}) async-start(bf16[4,32,192]{2,1,0:T(8,128)(2,1)} %bitcast.73), calls=%async_computation.4 | async-start | bytes 131072 | tf_op jit(solution)/shard_map/all_to_all | solution.py:46
